TPU v7x, 32 devices: a whole 2x2x4 slice. The times are simulated.
32 devices in a mesh: groups: 2 (over x), blk: 8 (over z, y), head: 2 (over core).
Axes of the slice: x: 2, y: 2, z: 4, core: 2. Of those that a mesh axis runs over, the one named last changes fastest.
Arguments:
- q_latent: float32 [32, 128, 512], P(('groups', 'blk'), 'head'), parts along dimension 0, may hold values from -16 to 16
- q_rope: float32 [32, 128, 64], P(('groups', 'blk'), 'head'), parts along dimension 0, may hold values from -8 to 8
- cache_latent: float32 [32768, 512], P(('groups', 'blk')), parts along dimension 0, may hold values from -8 to 8
- cache_rope: float32 [32768, 64], P(('groups', 'blk')), parts along dimension 0, may hold values from -4 to 4
- home_offset: int32 [32], P(('groups', 'blk')), parts along dimension 0, may hold values from 0 to 14335
- lengths: int32 [32], P(('groups', 'blk')), parts along dimension 0, may hold values from 1 to 14336, as said below
Outputs:
- attended: float32 [32, 128, 512], P(('groups', 'blk'), 'head'), parts along dimension 0
There are 2 independent parts, one for each index of `groups`. A program takes and returns all parts, laid end to end along the dimension named above; each array names one. Nothing has to cross between parts.
Inputs may be any that keep to these rules, and one draw needn't show every extreme that they name: `lengths`: some query has all 14336 cells live.
All inputs are finite; a program needn't handle non-finite values.
Results may differ from a plain program's by a relative error of at most 0.0003.
Values sent between devices are 32-bit elements; how exact they have to be, the bound alone decides.
A program may use at most 64 MiB of HBM per device.

v0:
```python
import math

import jax
import jax.numpy as jnp
from jax import lax
from jax.sharding import PartitionSpec as P

ROPE = 64
NOPE = 128
HOPS = 3


precise = lax.Precision.HIGHEST
floor_value = -1e30


def from_behind(x, axis, by):
    size = lax.axis_size(axis)
    return lax.ppermute(x, axis, [(i, (i + by) % size) for i in range(size)])


def visit_block(
    queries, rope_part, beginnings, extents, window_slot, latent_cache, rope_cache, carried
):
    peak_old, totals, summed = carried
    height, head_count, latent_width = queries.shape
    cell_count = latent_cache.shape[0]
    window_size = (2 * HOPS + 1) * cell_count
    scale = 1.0 / math.sqrt(NOPE + ROPE)
    flat_query = queries.reshape(height * head_count, latent_width)
    flat_rope = rope_part.reshape(height * head_count, rope_part.shape[2])
    scores = (
        jnp.dot(flat_query, latent_cache.T, precision=precise)
        + jnp.dot(flat_rope, rope_cache.T, precision=precise)
    ) * scale
    scores = scores.reshape(height, head_count, cell_count)
    offsets = window_slot[:, None] * cell_count + jnp.arange(cell_count, dtype=jnp.int32)[None, :]
    validity = (jnp.mod(offsets - beginnings[:, None], window_size) < extents[:, None])[:, None, :]
    local_peak = jnp.max(jnp.where(validity, scores, floor_value), axis=2)
    peak = jnp.maximum(peak_old, local_peak)
    weights = jnp.where(validity, jnp.exp(scores - peak[:, :, None]), 0.0)
    fading = jnp.exp(peak_old - peak)
    totals = totals * fading + jnp.sum(weights, axis=2)
    product = jnp.dot(
        weights.reshape(height * head_count, cell_count), latent_cache, precision=precise
    )
    summed = summed * fading[:, :, None] + product.reshape(height, head_count, latent_width)
    return (peak, totals, summed)


def combine_parts(first, second):
    peak = jnp.maximum(first[0], second[0])
    first_scale = jnp.exp(first[0] - peak)
    second_scale = jnp.exp(second[0] - peak)
    totals = first[1] * first_scale + second[1] * second_scale
    summed = first[2] * first_scale[:, :, None] + second[2] * second_scale[:, :, None]
    return (peak, totals, summed)


def as_index(values):
    return values.astype(jnp.int32)


def pass_onward(parcel):
    return from_behind(parcel, "blk", 1)


def send_homeward(parcel):
    return from_behind(parcel, "blk", -HOPS)


def shards(q_latent, q_rope, cache_latent, cache_rope, home_offset, lengths):
    height, head_count, latent_width = q_latent.shape
    start_float = home_offset.astype(jnp.float32)
    extent_float = lengths.astype(jnp.float32)
    empty = (
        jnp.full((height, head_count), floor_value, jnp.float32),
        jnp.zeros((height, head_count), jnp.float32),
        jnp.zeros((height, head_count, latent_width), jnp.float32),
    )
    window_slot = jnp.full((height,), HOPS, jnp.int32)
    upward = visit_block(
        q_latent, q_rope, home_offset, lengths, window_slot, cache_latent, cache_rope, empty
    )
    up_parcel = (q_latent, q_rope, start_float, extent_float) + upward
    down_parcel = (q_latent, q_rope, start_float, extent_float) + empty
    for hop_index in range(1, HOPS + 1):
        up_parcel = pass_onward(up_parcel)
        down_parcel = from_behind(down_parcel, "blk", -1)
        slots = jnp.concatenate(
            [
                jnp.full((height,), HOPS + hop_index, jnp.int32),
                jnp.full((height,), HOPS - hop_index, jnp.int32),
            ]
        )
        joined = tuple(
            (
                jnp.concatenate([upper, lower], axis=0)
                for upper, lower in zip(up_parcel, down_parcel)
            )
        )
        carried = visit_block(
            joined[0],
            joined[1],
            as_index(joined[2]),
            as_index(joined[3]),
            slots,
            cache_latent,
            cache_rope,
            joined[4:],
        )
        up_parcel = tuple(up_parcel[:4]) + tuple((part_value[:height] for part_value in carried))
        down_parcel = tuple(down_parcel[:4]) + tuple(
            (part_value[height:] for part_value in carried)
        )
    upper_done = send_homeward(up_parcel[4:])
    lower_done = from_behind(down_parcel[4:], "blk", HOPS)
    peak, totals, summed = combine_parts(upper_done, lower_done)
    return summed / totals[:, :, None]


def solution(mesh):
    return jax.shard_map(
        shards,
        mesh=mesh,
        in_specs=(
            P(("groups", "blk"), "head", None),
            P(("groups", "blk"), "head", None),
            P(("groups", "blk"), None),
            P(("groups", "blk"), None),
            P(("groups", "blk")),
            P(("groups", "blk")),
        ),
        out_specs=P(("groups", "blk"), "head", None),
        check_vma=False,
    )
```

profile of v0, /device:TPU:8, one launch (start us, length us, event | category | flops | bytes accessed | tf_op | source)
XLA Modules:
  0.0 218.2 jit_solution(9556441695872098299)
XLA Ops:
  9.4 6.6 %fusion.59 = f32[128,2048]{1,0:T(8,128)S(1)} fusion(f32[128,512]{1,0:T(8,128)} %bitcast.1, f32[2048,512]{1,0:T(8,128)} %param.8), kind=kOutput, calls=%fused_computation.108 | convolution fusion | flops 1610612736 | bytes 5505024 | tf_op jit(solution)/shard_map/dot_general | solution.py:33
  17.8 4.7 %fusion.15 = f32[2,64,512]{2,1,0:T(8,128)S(1)} fusion(f32[2,64,2048]{2,1,0:T(8,128)S(1)} %bitcast.88, f32[2048,512]{1,0:T(8,128)} %param.8, f32[2,64]{1,0:T(2,128)S(1)} %get-tuple-element.44), kind=kOutput, calls=%fused_computation.27 | convolution fusion | flops 1610678272 | bytes 5505536 | tf_op jit(solution)/shard_map/dot_general | solution.py:44
  22.7 3.9 %collective-permute-start.9 = (f32[2,64,512]{2,1,0:T(8,128)}, f32[2,64,512]{2,1,0:T(8,128)}, u32[]{:S(2)}, u32[]{:S(2)}) collective-permute-start(f32[2,64,512]{2,1,0:T(8,128)} %param.6), channel_id=1, source_target_pairs={{0,14},{2,0},{4,2},{6,4},{8,6},{10,8},{12,10},{14,12},{1,15},{3,1}... | collective-permute-start | bytes 786440 | tf_op jit(solution)/shard_map/ppermute | solution.py:19
  26.9 4.8 %collective-permute-start.19 = (f32[2]{0:T(128)S(1)}, f32[2]{0:T(128)S(1)}, u32[]{:S(2)}, u32[]{:S(2)}) collective-permute-start(f32[2]{0:T(128)S(1)} %collective-permute-done.7), channel_id=1, source_target_pairs={{0,14},{2,0},{4,2},{6,4},{8,6},{10,8},{12,10},{14,12},{1,15},{3,1}... | collective-permute-start | bytes 32 | tf_op jit(solution)/shard_map/ppermute | solution.py:19
  33.3 5.8 %collective-permute-done.18 = f32[2]{0:T(128)S(1)} collective-permute-done((f32[2]{0:T(128)S(1)}, f32[2]{0:T(128)S(1)}, u32[]{:S(2)}, u32[]{:S(2)}) %collective-permute-start.18) | collective-permute-done | bytes 40 | tf_op jit(solution)/shard_map/ppermute | solution.py:19
  39.1 4.7 %collective-permute-start.17 = (f32[2]{0:T(128)S(1)}, f32[2]{0:T(128)S(1)}, u32[]{:S(2)}, u32[]{:S(2)}) collective-permute-start(f32[2]{0:T(128)S(1)} %collective-permute-done.5), channel_id=1, source_target_pairs={{0,14},{2,0},{4,2},{6,4},{8,6},{10,8},{12,10},{14,12},{1,15},{3,1}... | collective-permute-start | bytes 32 | tf_op jit(solution)/shard_map/ppermute | solution.py:19
  45.1 6.5 %collective-permute-done.16 = f32[2]{0:T(128)S(1)} collective-permute-done((f32[2]{0:T(128)S(1)}, f32[2]{0:T(128)S(1)}, u32[]{:S(2)}, u32[]{:S(2)}) %collective-permute-start.16) | collective-permute-done | bytes 40 | tf_op jit(solution)/shard_map/ppermute | solution.py:19
  55.5 6.3 %collective-permute-done.30 = f32[2]{0:T(128)S(1)} collective-permute-done((f32[2]{0:T(128)S(1)}, f32[2]{0:T(128)S(1)}, u32[]{:S(2)}, u32[]{:S(2)}) %collective-permute-start.30) | collective-permute-done | bytes 40 | tf_op jit(solution)/shard_map/ppermute | solution.py:19
  65.3 6.3 %collective-permute-done.28 = f32[2]{0:T(128)S(1)} collective-permute-done((f32[2]{0:T(128)S(1)}, f32[2]{0:T(128)S(1)}, u32[]{:S(2)}, u32[]{:S(2)}) %collective-permute-start.28) | collective-permute-done | bytes 40 | tf_op jit(solution)/shard_map/ppermute | solution.py:19
  71.7 4.5 %collective-permute-start.3 = (f32[2,64]{1,0:T(2,128)S(1)}, f32[2,64]{1,0:T(2,128)S(1)}, u32[]{:S(2)}, u32[]{:S(2)}) collective-permute-start(f32[2,64]{1,0:T(2,128)S(1)} %broadcast_in_dim.102), channel_id=1, source_target_pairs={{0,14},{2,0},{4,2},{6,4},{8,6},{10,8},{12,10},{14,12},{1,15},{3,1}... | collective-permute-start | bytes 1544 | tf_op jit(solution)/shard_map/ppermute | solution.py:19
  85.4 6.4 %collective-permute-done.23 = f32[2,64,64]{2,1,0:T(8,128)S(1)} collective-permute-done((f32[2,64,64]{2,1,0:T(8,128)S(1)}, f32[2,64,64]{2,1,0:T(8,128)S(1)}, u32[]{:S(2)}, u32[]{:S(2)}) %collective-permute-start.23) | collective-permute-done | bytes 32800 | tf_op jit(solution)/shard_map/ppermute | solution.py:19
  91.8 3.4 %collective-permute-start.35 = (f32[2,64,64]{2,1,0:T(8,128)S(1)}, f32[2,64,64]{2,1,0:T(8,128)S(1)}, u32[]{:S(2)}, u32[]{:S(2)}) collective-permute-start(f32[2,64,64]{2,1,0:T(8,128)S(1)} %collective-permute-done.23), channel_id=1, source_target_pairs={{0,14},{2,0},{4,2},{6,4},{8,6},{10,8},{12,10},{14,12},{1,15},{3,1}... | collective-permute-start | bytes 98312 | tf_op jit(solution)/shard_map/ppermute | solution.py:19
  105.7 5.2 %fusion.12 = (f32[256]{0:T(256)S(1)}, f32[256,2048]{1,0:T(8,128)}) fusion(pred[4,2048]{1,0:T(4,128)(4,1)S(1)} %fusion.22, f32[256,2048]{1,0:T(8,128)S(1)} %fusion.60, f32[256,512]{1,0:T(8,128)S(1)} %bitcast.90, f32[2048,512]{1,0:T(8,128)S(1)} %copy-done.1), kind=kOutput, calls=%fused_computation.22 | convolution fusion | flops 3223322368 | bytes 8922112 | tf_op jit(solution)/shard_map/dot_general | solution.py:33
  111.0 3.4 %fusion.47 = (f32[256]{0:T(256)S(1)}, f32[256,2048]{1,0:T(8,128)}) fusion(f32[256,2048]{1,0:T(8,128)} %get-tuple-element.48, f32[256]{0:T(256)S(1)} %max.40, pred[4,2048]{1,0:T(4,128)(4,1)S(1)} %fusion.22), kind=kLoop, calls=%fused_computation.96 | loop fusion | flops 1572608 | bytes 4204544 | tf_op jit(solution)/shard_map/reduce_sum | solution.py:43
  114.5 6.3 %fusion.19 = f32[4,64,512]{2,1,0:T(8,128)S(1)} fusion(f32[2,64,512]{2,1,0:T(8,128)S(1)} %collective-permute-done.1, f32[2,64,512]{2,1,0:T(8,128)S(1)} %collective-permute-done, f32[4,64]{1,0:T(4,128)S(1)} %get-tuple-element.13, f32[4,64,2048]{2,1,0:T(8,128)} %bitcast.85, f32[2048,512]{1,0:T(8,128)} %param.8), kind=kOutput, calls=%fused_computation.30 | convolution fusion | flops 3221618688 | bytes 7341056 | tf_op jit(solution)/shard_map/dot_general | solution.py:44
  126.8 4.7 %collective-permute-start.21 = (f32[2,64,512]{2,1,0:T(8,128)}, f32[2,64,512]{2,1,0:T(8,128)}, u32[]{:S(2)}, u32[]{:S(2)}) collective-permute-start(f32[2,64,512]{2,1,0:T(8,128)} %collective-permute-done.9), channel_id=1, source_target_pairs={{0,14},{2,0},{4,2},{6,4},{8,6},{10,8},{12,10},{14,12},{1,15},{3,1}... | collective-permute-start | bytes 786440 | tf_op jit(solution)/shard_map/ppermute | solution.py:19
  140.0 12.4 %fusion.13 = (f32[256]{0:T(256)S(1)}, f32[256,2048]{1,0:T(8,128)}) fusion(pred[4,2048]{1,0:T(4,128)(4,1)S(1)} %fusion.23, f32[256,2048]{1,0:T(8,128)} %fusion.61, f32[256,512]{1,0:T(8,128)S(1)} %bitcast.91, f32[2048,512]{1,0:T(8,128)} %param.8), kind=kOutput, calls=%fused_computation.23 | convolution fusion | flops 3223322368 | bytes 8922112 | tf_op jit(solution)/shard_map/dot_general | solution.py:33
  152.5 3.4 %fusion.48 = (f32[256]{0:T(256)S(1)}, f32[256,2048]{1,0:T(8,128)}) fusion(f32[256,2048]{1,0:T(8,128)} %get-tuple-element.50, f32[256]{0:T(256)S(1)} %max.42, pred[4,2048]{1,0:T(4,128)(4,1)S(1)} %fusion.23), kind=kLoop, calls=%fused_computation.97 | loop fusion | flops 1572608 | bytes 4204544 | tf_op jit(solution)/shard_map/reduce_sum | solution.py:43
  156.0 6.3 %fusion.20 = f32[4,64,512]{2,1,0:T(8,128)S(1)} fusion(f32[2,64,512]{2,1,0:T(8,128)S(1)} %collective-permute-done.13, f32[2,64,512]{2,1,0:T(8,128)S(1)} %collective-permute-done.12, f32[4,64]{1,0:T(4,128)S(1)} %get-tuple-element.11, f32[4,64,2048]{2,1,0:T(8,128)} %bitcast.86, f32[2048,512]{1,0:T(8,128)} %param.8), kind=kOutput, calls=%fused_computation.33 | convolution fusion | flops 3221618688 | bytes 7341056 | tf_op jit(solution)/shard_map/dot_general | solution.py:44
  165.9 3.7 %collective-permute-start.27 = (f32[2,64]{1,0:T(2,128)S(1)}, f32[2,64]{1,0:T(2,128)S(1)}, u32[]{:S(2)}, u32[]{:S(2)}) collective-permute-start(f32[2,64]{1,0:T(2,128)S(1)} %get-tuple-element.40), channel_id=1, source_target_pairs={{0,14},{2,0},{4,2},{6,4},{8,6},{10,8},{12,10},{14,12},{1,15},{3,1}... | collective-permute-start | bytes 1544 | tf_op jit(solution)/shard_map/ppermute | solution.py:19
  181.0 7.3 %fusion.14 = (f32[256]{0:T(256)S(1)}, f32[256,2048]{1,0:T(8,128)}) fusion(pred[4,2048]{1,0:T(4,128)(4,1)S(1)} %fusion.24, f32[256,2048]{1,0:T(8,128)S(1)} %fusion.62, f32[256,512]{1,0:T(8,128)S(1)} %bitcast.89, f32[2048,512]{1,0:T(8,128)} %param.8), kind=kOutput, calls=%fused_computation.24 | convolution fusion | flops 3223322368 | bytes 8922112 | tf_op jit(solution)/shard_map/dot_general | solution.py:33
  190.6 5.6 %fusion.21 = f32[4,64,512]{2,1,0:T(8,128)S(1)} fusion(f32[2,64,512]{2,1,0:T(8,128)S(1)} %collective-permute-done.25, f32[2,64,512]{2,1,0:T(8,128)S(1)} %collective-permute-done.24, f32[4,64]{1,0:T(4,128)S(1)} %get-tuple-element.9, f32[4,64,2048]{2,1,0:T(8,128)S(1)} %bitcast.87, f32[2048,512]{1,0:T(8,128)} %param.8), kind=kOutput, calls=%fused_computation.36 | convolution fusion | flops 3221618688 | bytes 7341056 | tf_op jit(solution)/shard_map/dot_general | solution.py:44
  196.3 6.1 %collective-permute-start.39 = (f32[2,64,512]{2,1,0:T(8,128)S(1)}, f32[2,64,512]{2,1,0:T(8,128)S(1)}, u32[]{:S(2)}, u32[]{:S(2)}) collective-permute-start(f32[2,64,512]{2,1,0:T(8,128)S(1)} %get-tuple-element.23), channel_id=1, source_target_pairs={{0,6},{2,8},{4,10},{6,12},{8,14},{10,0},{12,2},{14,4},{1,7},{3,9},... | collective-permute-start | bytes 786440 | tf_op jit(solution)/shard_map/ppermute | solution.py:19
  206.3 5.7 %collective-permute-done.47 = f32[2,64]{1,0:T(2,128)S(1)} collective-permute-done((f32[2,64]{1,0:T(2,128)S(1)}, f32[2,64]{1,0:T(2,128)S(1)}, u32[]{:S(2)}, u32[]{:S(2)}) %collective-permute-start.47) | collective-permute-done | bytes 544 | tf_op jit(solution)/shard_map/ppermute | solution.py:19
  (155 shorter events, 83.8 us)
Async XLA Ops:
  0.7 21.8 %collective-permute-start.7 = (f32[2]{0:T(128)S(1)}, f32[2]{0:T(128)S(1)}, u32[]{:S(2)}, u32[]{:S(2)}) collective-permute-start(f32[2]{0:T(128)S(1)} %convert_element_type.50), channel_id=1, source_target_pairs={{0,14},{2,0},{4,2},{6,4},{8,6},{10,8},{12,10},{14,12},{1,15},{3,1}... | collective-permute-start | bytes 32 | tf_op jit(solution)/shard_map/ppermute | solution.py:19
  2.1 20.5 %collective-permute-start.6 = (f32[2]{0:T(128)S(1)}, f32[2]{0:T(128)S(1)}, u32[]{:S(2)}, u32[]{:S(2)}) collective-permute-start(f32[2]{0:T(128)S(1)} %convert_element_type.50), channel_id=1, source_target_pairs={{0,2},{2,4},{4,6},{6,8},{8,10},{10,12},{12,14},{14,0},{1,3},{3,5},... | collective-permute-start | bytes 32 | tf_op jit(solution)/shard_map/ppermute | solution.py:19
  3.4 23.2 %collective-permute-start.5 = (f32[2]{0:T(128)S(1)}, f32[2]{0:T(128)S(1)}, u32[]{:S(2)}, u32[]{:S(2)}) collective-permute-start(f32[2]{0:T(128)S(1)} %convert_element_type.48), channel_id=1, source_target_pairs={{0,14},{2,0},{4,2},{6,4},{8,6},{10,8},{12,10},{14,12},{1,15},{3,1}... | collective-permute-start | bytes 32 | tf_op jit(solution)/shard_map/ppermute | solution.py:19
  5.7 20.9 %collective-permute-start.4 = (f32[2]{0:T(128)S(1)}, f32[2]{0:T(128)S(1)}, u32[]{:S(2)}, u32[]{:S(2)}) collective-permute-start(f32[2]{0:T(128)S(1)} %convert_element_type.48), channel_id=1, source_target_pairs={{0,2},{2,4},{4,6},{6,8},{8,10},{10,12},{12,14},{14,0},{1,3},{3,5},... | collective-permute-start | bytes 32 | tf_op jit(solution)/shard_map/ppermute | solution.py:19
  5.8 75.7 %collective-permute-start.11 = (f32[2,64,64]{2,1,0:T(8,128)}, f32[2,64,64]{2,1,0:T(8,128)S(1)}, u32[]{:S(2)}, u32[]{:S(2)}) collective-permute-start(f32[2,64,64]{2,1,0:T(8,128)} %param.7), channel_id=1, source_target_pairs={{0,14},{2,0},{4,2},{6,4},{8,6},{10,8},{12,10},{14,12},{1,15},{3,1}... | collective-permute-start | bytes 98312 | tf_op jit(solution)/shard_map/ppermute | solution.py:19
  22.5 61.0 %collective-permute-start.10 = (f32[2,64,64]{2,1,0:T(8,128)S(1)}, f32[2,64,64]{2,1,0:T(8,128)S(1)}, u32[]{:S(2)}, u32[]{:S(2)}) collective-permute-start(f32[2,64,64]{2,1,0:T(8,128)S(1)} %copy-done.2), channel_id=1, source_target_pairs={{0,2},{2,4},{4,6},{6,8},{8,10},{10,12},{12,14},{14,0},{1,3},{3,5},... | collective-permute-start | bytes 98312 | tf_op jit(solution)/shard_map/ppermute | solution.py:19
  22.7 81.4 %collective-permute-start.9 = (f32[2,64,512]{2,1,0:T(8,128)}, f32[2,64,512]{2,1,0:T(8,128)}, u32[]{:S(2)}, u32[]{:S(2)}) collective-permute-start(f32[2,64,512]{2,1,0:T(8,128)} %param.6), channel_id=1, source_target_pairs={{0,14},{2,0},{4,2},{6,4},{8,6},{10,8},{12,10},{14,12},{1,15},{3,1}... | collective-permute-start | bytes 786440 | tf_op jit(solution)/shard_map/ppermute | solution.py:19
  26.6 50.8 %collective-permute-start.2 = (f32[2,64]{1,0:T(2,128)S(1)}, f32[2,64]{1,0:T(2,128)S(1)}, u32[]{:S(2)}, u32[]{:S(2)}) collective-permute-start(f32[2,64]{1,0:T(2,128)S(1)} %max_broadcast_in_dim.14), channel_id=1, source_target_pairs={{0,2},{2,4},{4,6},{6,8},{8,10},{10,12},{12,14},{14,0},{1,3},{3,5},... | collective-permute-start | bytes 1544 | tf_op jit(solution)/shard_map/ppermute | solution.py:19
  77.5 27.1 %collective-permute-start.8 = (f32[2,64,512]{2,1,0:T(8,128)}, f32[2,64,512]{2,1,0:T(8,128)}, u32[]{:S(2)}, u32[]{:S(2)}) collective-permute-start(f32[2,64,512]{2,1,0:T(8,128)} %param.6), channel_id=1, source_target_pairs={{0,2},{2,4},{4,6},{6,8},{8,10},{10,12},{12,14},{14,0},{1,3},{3,5},... | collective-permute-start | bytes 786440 | tf_op jit(solution)/shard_map/ppermute | solution.py:19
  78.2 36.3 %collective-permute-start.1 = (f32[2,64,512]{2,1,0:T(8,128)}, f32[2,64,512]{2,1,0:T(8,128)S(1)}, u32[]{:S(2)}, u32[]{:S(2)}) collective-permute-start(f32[2,64,512]{2,1,0:T(8,128)} %broadcast_in_dim.109), channel_id=1, source_target_pairs={{0,14},{2,0},{4,2},{6,4},{8,6},{10,8},{12,10},{14,12},{1,15},{3,1}... | collective-permute-start | bytes 786440 | tf_op jit(solution)/shard_map/ppermute | solution.py:19
  83.5 11.7 %collective-permute-start.22 = (f32[2,64,64]{2,1,0:T(8,128)S(1)}, f32[2,64,64]{2,1,0:T(8,128)S(1)}, u32[]{:S(2)}, u32[]{:S(2)}) collective-permute-start(f32[2,64,64]{2,1,0:T(8,128)S(1)} %collective-permute-done.10), channel_id=1, source_target_pairs={{0,2},{2,4},{4,6},{6,8},{8,10},{10,12},{12,14},{14,0},{1,3},{3,5},... | collective-permute-start | bytes 98312 | tf_op jit(solution)/shard_map/ppermute | solution.py:19
  98.7 15.8 %collective-permute-start = (f32[2,64,512]{2,1,0:T(8,128)S(1)}, f32[2,64,512]{2,1,0:T(8,128)S(1)}, u32[]{:S(2)}, u32[]{:S(2)}) collective-permute-start(f32[2,64,512]{2,1,0:T(8,128)S(1)} %fusion.15), channel_id=1, source_target_pairs={{0,2},{2,4},{4,6},{6,8},{8,10},{10,12},{12,14},{14,0},{1,3},{3,5},... | collective-permute-start | bytes 786440 | tf_op jit(solution)/shard_map/ppermute | solution.py:19
  100.7 13.8 %collective-permute-start.41 = (f32[2,64]{1,0:T(2,128)S(1)}, f32[2,64]{1,0:T(2,128)S(1)}, u32[]{:S(2)}, u32[]{:S(2)}) collective-permute-start(f32[2,64]{1,0:T(2,128)S(1)} %broadcast_in_dim.107), channel_id=1, source_target_pairs={{0,14},{2,0},{4,2},{6,4},{8,6},{10,8},{12,10},{14,12},{1,15},{3,1}... | collective-permute-start | bytes 1544 | tf_op jit(solution)/shard_map/ppermute | solution.py:19
  104.1 10.4 %collective-permute-start.40 = (f32[2,64]{1,0:T(2,128)S(1)}, f32[2,64]{1,0:T(2,128)S(1)}, u32[]{:S(2)}, u32[]{:S(2)}) collective-permute-start(f32[2,64]{1,0:T(2,128)S(1)} %get-tuple-element.43), channel_id=1, source_target_pairs={{0,2},{2,4},{4,6},{6,8},{8,10},{10,12},{12,14},{14,0},{1,3},{3,5},... | collective-permute-start | bytes 1544 | tf_op jit(solution)/shard_map/ppermute | solution.py:19
  121.6 34.4 %collective-permute-start.13 = (f32[2,64,512]{2,1,0:T(8,128)}, f32[2,64,512]{2,1,0:T(8,128)S(1)}, u32[]{:S(2)}, u32[]{:S(2)}) collective-permute-start(f32[2,64,512]{2,1,0:T(8,128)} %get-tuple-element.27), channel_id=1, source_target_pairs={{0,14},{2,0},{4,2},{6,4},{8,6},{10,8},{12,10},{14,12},{1,15},{3,1}... | collective-permute-start | bytes 786440 | tf_op jit(solution)/shard_map/ppermute | solution.py:19
  131.5 24.4 %collective-permute-start.12 = (f32[2,64,512]{2,1,0:T(8,128)}, f32[2,64,512]{2,1,0:T(8,128)S(1)}, u32[]{:S(2)}, u32[]{:S(2)}) collective-permute-start(f32[2,64,512]{2,1,0:T(8,128)} %get-tuple-element.26), channel_id=1, source_target_pairs={{0,2},{2,4},{4,6},{6,8},{8,10},{10,12},{12,14},{14,0},{1,3},{3,5},... | collective-permute-start | bytes 786440 | tf_op jit(solution)/shard_map/ppermute | solution.py:19
  133.1 22.9 %collective-permute-start.43 = (f32[2,64]{1,0:T(2,128)S(1)}, f32[2,64]{1,0:T(2,128)S(1)}, u32[]{:S(2)}, u32[]{:S(2)}) collective-permute-start(f32[2,64]{1,0:T(2,128)S(1)} %get-tuple-element.38), channel_id=1, source_target_pairs={{0,14},{2,0},{4,2},{6,4},{8,6},{10,8},{12,10},{14,12},{1,15},{3,1}... | collective-permute-start | bytes 1544 | tf_op jit(solution)/shard_map/ppermute | solution.py:19
  135.7 20.2 %collective-permute-start.42 = (f32[2,64]{1,0:T(2,128)S(1)}, f32[2,64]{1,0:T(2,128)S(1)}, u32[]{:S(2)}, u32[]{:S(2)}) collective-permute-start(f32[2,64]{1,0:T(2,128)S(1)} %get-tuple-element.37), channel_id=1, source_target_pairs={{0,2},{2,4},{4,6},{6,8},{8,10},{10,12},{12,14},{14,0},{1,3},{3,5},... | collective-permute-start | bytes 1544 | tf_op jit(solution)/shard_map/ppermute | solution.py:19
  163.1 27.5 %collective-permute-start.25 = (f32[2,64,512]{2,1,0:T(8,128)}, f32[2,64,512]{2,1,0:T(8,128)S(1)}, u32[]{:S(2)}, u32[]{:S(2)}) collective-permute-start(f32[2,64,512]{2,1,0:T(8,128)} %get-tuple-element.25), channel_id=1, source_target_pairs={{0,14},{2,0},{4,2},{6,4},{8,6},{10,8},{12,10},{14,12},{1,15},{3,1}... | collective-permute-start | bytes 786440 | tf_op jit(solution)/shard_map/ppermute | solution.py:19
  172.6 18.0 %collective-permute-start.24 = (f32[2,64,512]{2,1,0:T(8,128)}, f32[2,64,512]{2,1,0:T(8,128)S(1)}, u32[]{:S(2)}, u32[]{:S(2)}) collective-permute-start(f32[2,64,512]{2,1,0:T(8,128)} %get-tuple-element.24), channel_id=1, source_target_pairs={{0,2},{2,4},{4,6},{6,8},{8,10},{10,12},{12,14},{14,0},{1,3},{3,5},... | collective-permute-start | bytes 786440 | tf_op jit(solution)/shard_map/ppermute | solution.py:19
  174.1 16.5 %collective-permute-start.45 = (f32[2,64]{1,0:T(2,128)S(1)}, f32[2,64]{1,0:T(2,128)S(1)}, u32[]{:S(2)}, u32[]{:S(2)}) collective-permute-start(f32[2,64]{1,0:T(2,128)S(1)} %get-tuple-element.36), channel_id=1, source_target_pairs={{0,14},{2,0},{4,2},{6,4},{8,6},{10,8},{12,10},{14,12},{1,15},{3,1}... | collective-permute-start | bytes 1544 | tf_op jit(solution)/shard_map/ppermute | solution.py:19
  176.8 13.8 %collective-permute-start.44 = (f32[2,64]{1,0:T(2,128)S(1)}, f32[2,64]{1,0:T(2,128)S(1)}, u32[]{:S(2)}, u32[]{:S(2)}) collective-permute-start(f32[2,64]{1,0:T(2,128)S(1)} %get-tuple-element.35), channel_id=1, source_target_pairs={{0,2},{2,4},{4,6},{6,8},{8,10},{10,12},{12,14},{14,0},{1,3},{3,5},... | collective-permute-start | bytes 1544 | tf_op jit(solution)/shard_map/ppermute | solution.py:19
  196.3 21.0 %collective-permute-start.39 = (f32[2,64,512]{2,1,0:T(8,128)S(1)}, f32[2,64,512]{2,1,0:T(8,128)S(1)}, u32[]{:S(2)}, u32[]{:S(2)}) collective-permute-start(f32[2,64,512]{2,1,0:T(8,128)S(1)} %get-tuple-element.23), channel_id=1, source_target_pairs={{0,6},{2,8},{4,10},{6,12},{8,14},{10,0},{12,2},{14,4},{1,7},{3,9},... | collective-permute-start | bytes 786440 | tf_op jit(solution)/shard_map/ppermute | solution.py:19
  202.4 15.0 %collective-permute-start.36 = (f32[2,64,512]{2,1,0:T(8,128)S(1)}, f32[2,64,512]{2,1,0:T(8,128)S(1)}, u32[]{:S(2)}, u32[]{:S(2)}) collective-permute-start(f32[2,64,512]{2,1,0:T(8,128)S(1)} %get-tuple-element.22), channel_id=1, source_target_pairs={{0,10},{2,12},{4,14},{6,0},{8,2},{10,4},{12,6},{14,8},{1,11},{3,13... | collective-permute-start | bytes 786440 | tf_op jit(solution)/shard_map/ppermute | solution.py:19
  (30 other events, 296.9 us)
where the time goes:
time: 221 us; the launch traced here: 218 us
  starting transfers between devices  77.6 us (35%)
  matrix products  62.2 us (28%)
  waiting for transfers between devices  58.3 us (26%)
  other arithmetic  16.3 us (7%)
  local copies, waits for them, and re-layouts  3.41 us (2%)
    ppermute x48, starting transfers between devices, from_behind(): return lax.ppermute(x, axis, [(i, (i + by) % size) for i in range(size)])  77.6 us
    ppermute x48, waiting for transfers between devices, from_behind(): return lax.ppermute(x, axis, [(i, (i + by) % size) for i in range(size)])  58.3 us
    dot_general x4, matrix products, visit_block(): jnp.dot(flat_query, latent_cache.T, precision=precise)  31.5 us
    dot_general x4, matrix products, visit_block(): jnp.dot(weights.reshape(height * head_count, cell_count), latent_cache, p...  22.8 us
    reduce_sum x4, other arithmetic, visit_block(): totals = totals * fading + jnp.sum(weights, axis=2)  9.23 us
    dot_general x4, matrix products, visit_block(): jnp.dot(flat_rope, rope_cache.T, precision=precise)  7.87 us
  transfers between devices with their start and end apart: 48, of which 19 were waited for; matrix products, arithmetic and copies ran while one was open for 28% of the time, Pallas kernels for 0%

commit v1 on v0

v1 whole, which is shorter than its diff:
```python
import functools
import math

import jax
import jax.numpy as jnp
from jax import lax
from jax.experimental import pallas as pl
from jax.experimental.pallas import tpu as pltpu
from jax.sharding import PartitionSpec as P

ROPE = 64
NOPE = 128
HOPS = 3

MESH = pl.DeviceIdType.MESH
FLOOR = -1e30
DEAD = -2e30
FACTOR = math.log2(math.e) / math.sqrt(NOPE + ROPE)
CHUNK = 512

NT = (((1,), (1,)), ((), ()))


def split(x):
    high = x.astype(jnp.bfloat16)
    low = (x - high.astype(jnp.float32)).astype(jnp.bfloat16)
    return high, low


def prepare_cache(cache_ref, rope_ref, kcat, vt_hi, vt_lo):
    cells, width = cache_ref.shape
    step = 256

    def body(i, _):
        rows = pl.ds(pl.multiple_of(i * step, step), step)
        block = cache_ref[rows, :]
        high, low = split(block)
        kcat[rows, 0:width] = high
        kcat[rows, width : 2 * width] = low
        turned = block.T
        t_high, t_low = split(turned)
        vt_hi[:, rows] = t_high
        vt_lo[:, rows] = t_low
        rope = rope_ref[rows, :]
        r_high = rope.astype(jnp.bfloat16).astype(jnp.float32)
        r_low = rope - r_high
        wide = jnp.concatenate([r_high, r_high, r_low, jnp.zeros_like(rope)], axis=1)
        kcat[rows, 2 * width : 2 * width + 4 * rope.shape[1]] = wide.astype(jnp.bfloat16)
        return 0

    lax.fori_loop(0, cells // step, body, 0)


def rope_rows(aux, heads):
    packed = aux[0:heads, :] * FACTOR
    high = packed.astype(jnp.bfloat16).astype(jnp.float32)
    low = packed - high
    half = packed.shape[1] // 2
    blank = jnp.zeros((heads, half), jnp.float32)
    rows = []
    for part in (slice(0, half), slice(half, 2 * half)):
        rows.append(jnp.concatenate([high[:, part], low[:, part], high[:, part], blank], axis=1))
    return jnp.concatenate(rows, axis=0).astype(jnp.bfloat16)


def visit(parts, kcat, vt_hi, vt_lo, s_ref, ph_ref, pl_ref, window):
    cells = kcat.shape[0]
    width = vt_hi.shape[0]
    heads = parts[0][1].shape[0] - 8
    query = jnp.concatenate([p[0] for p in parts], axis=0) * FACTOR
    q_hi, q_lo = split(query)
    rope = jnp.concatenate([rope_rows(p[1], heads) for p in parts], axis=0)
    q_cat = jnp.concatenate([q_hi, q_hi, rope], axis=1)
    starts = jnp.concatenate([p[1][heads : heads + 1, :] - p[2] for p in parts], axis=1)
    extents = jnp.concatenate([p[1][heads + 1 : heads + 2, :] for p in parts], axis=1)
    ends = starts + extents
    wrapped = ends - window
    count = query.shape[0]
    peak = jnp.full((1, count), FLOOR, jnp.float32)
    for c in range(cells // CHUNK):
        rows = slice(c * CHUNK, (c + 1) * CHUNK)
        scores = lax.dot_general(kcat[rows, :], q_cat, NT, preferred_element_type=jnp.float32)
        scores += lax.dot_general(
            kcat[rows, 0:width], q_lo, NT, preferred_element_type=jnp.float32
        )
        cell = lax.broadcasted_iota(jnp.int32, (CHUNK, count), 0).astype(jnp.float32) + c * CHUNK
        live = ((cell >= starts) & (cell < ends)) | (cell < wrapped)
        scores = jnp.where(live, scores, DEAD)
        s_ref[rows, 0:count] = scores
        peak = jnp.maximum(peak, jnp.max(scores, axis=0, keepdims=True))
    total = jnp.zeros((1, count), jnp.float32)
    summed = None
    for c in range(cells // CHUNK):
        rows = slice(c * CHUNK, (c + 1) * CHUNK)
        weights = jnp.exp2(s_ref[rows, 0:count] - peak)
        total += jnp.sum(weights, axis=0, keepdims=True)
        high, low = split(weights)
        ph_ref[rows, 0:count] = high
        pl_ref[rows, 0:count] = low
    high = ph_ref[:, 0:count]
    summed = jnp.dot(vt_hi[...], high, preferred_element_type=jnp.float32)
    summed += jnp.dot(vt_hi[...], pl_ref[:, 0:count], preferred_element_type=jnp.float32)
    summed += jnp.dot(vt_lo[...], high, preferred_element_type=jnp.float32)
    return summed, peak, total


def window_kernel(
    size,
    q_ref, aux_ref, cache_ref, rope_ref, out_ref,
    kcat, vt_hi, vt_lo, s_ref, ph_ref, pl_ref,
    q_got, aux_got, sums, stats, sums_got, stats_got,
    q_send, q_recv, a_send, a_recv, o_send, o_recv, t_send, t_recv,
):
    me = lax.axis_index("blk")
    cells = cache_ref.shape[0]
    window = (2 * HOPS + 1) * cells
    distances = [sign * k for k in range(1, HOPS + 1) for sign in (1, -1)]

    def device(distance):
        return {"blk": lax.rem(me + distance + size, size)}

    barrier = pltpu.get_barrier_semaphore()
    for d in distances:
        pl.semaphore_signal(barrier, inc=1, device_id=device(d), device_id_type=MESH)
    pl.semaphore_wait(barrier, 2 * HOPS)

    sent = []
    for i, d in enumerate(distances):
        for source, target, send, recv in (
            (q_ref, q_got, q_send, q_recv),
            (aux_ref, aux_got, a_send, a_recv),
        ):
            copy = pltpu.make_async_remote_copy(
                src_ref=source, dst_ref=target.at[i], send_sem=send.at[i], recv_sem=recv.at[i],
                device_id=device(d), device_id_type=MESH,
            )
            copy.start()
            sent.append(copy)

    prepare_cache(cache_ref, rope_ref, kcat, vt_hi, vt_lo)
    run = functools.partial(
        visit, kcat=kcat, vt_hi=vt_hi, vt_lo=vt_lo, s_ref=s_ref, ph_ref=ph_ref, pl_ref=pl_ref,
        window=window,
    )
    rows = q_ref.shape[0]
    own = run([(q_ref[...], aux_ref[...], float(HOPS * cells))])
    sums[2 * HOPS, :, :] = own[0]
    stats[2 * HOPS, 0:1, :] = own[1]
    stats[2 * HOPS, 1:2, :] = own[2]

    def pair(k, _):
        parts = []
        for j, sign in ((0, 1), (1, -1)):
            i = 2 * k + j
            for source, target, send, recv in (
                (q_ref, q_got, q_send, q_recv),
                (aux_ref, aux_got, a_send, a_recv),
            ):
                pltpu.make_async_remote_copy(
                    src_ref=source, dst_ref=target.at[i], send_sem=send.at[i], recv_sem=recv.at[i],
                    device_id=device(1), device_id_type=MESH,
                ).wait_recv()
            slot = HOPS + sign * (k + 1)
            parts.append((q_got[i], aux_got[i], (slot * cells).astype(jnp.float32)))
        summed, peak, total = run(parts)
        for j, sign in ((0, 1), (1, -1)):
            i = 2 * k + j
            lanes = slice(j * rows, (j + 1) * rows)
            sums[i, :, :] = summed[:, lanes]
            stats[i, 0:1, :] = peak[:, lanes]
            stats[i, 1:2, :] = total[:, lanes]
            for source, target, send, recv in (
                (sums, sums_got, o_send, o_recv),
                (stats, stats_got, t_send, t_recv),
            ):
                pltpu.make_async_remote_copy(
                    src_ref=source.at[i], dst_ref=target.at[i],
                    send_sem=send.at[i], recv_sem=recv.at[i],
                    device_id=device(-sign * (k + 1)), device_id_type=MESH,
                ).start()
        return 0

    lax.fori_loop(0, HOPS, pair, 0)

    for i in range(2 * HOPS):
        for source, target, send, recv in (
            (sums, sums_got, o_send, o_recv),
            (stats, stats_got, t_send, t_recv),
        ):
            copy = pltpu.make_async_remote_copy(
                src_ref=source.at[i], dst_ref=target.at[i],
                send_sem=send.at[i], recv_sem=recv.at[i],
                device_id=device(1), device_id_type=MESH,
            )
            copy.wait_recv()
            copy.wait_send()

    for copy in sent:
        copy.wait_send()

    peak = stats[2 * HOPS, 0:1, :]
    for i in range(2 * HOPS):
        peak = jnp.maximum(peak, stats_got[i, 0:1, :])
    factors = [jnp.exp2(stats[2 * HOPS, 0:1, :] - peak)]
    total = stats[2 * HOPS, 1:2, :] * factors[0]
    for i in range(2 * HOPS):
        factors.append(jnp.exp2(stats_got[i, 0:1, :] - peak))
        total += stats_got[i, 1:2, :] * factors[i + 1]
    width = sums.shape[1]
    for c in range(0, width, 128):
        piece = sums[2 * HOPS, c : c + 128, :] * factors[0]
        for i in range(2 * HOPS):
            piece += sums_got[i, c : c + 128, :] * factors[i + 1]
        out_ref[:, c : c + 128] = (piece / total).T


def pack_aux(q_rope, home_offset, lengths):
    height, heads, rope = q_rope.shape
    packed = jnp.concatenate([q_rope[i] for i in range(height)], axis=1)
    meta = jnp.stack([home_offset, lengths]).astype(jnp.float32)
    meta = jnp.repeat(meta, heads, axis=1)
    return jnp.concatenate([packed, meta, jnp.zeros((6, height * heads), jnp.float32)], axis=0)


def shards(size, q_latent, q_rope, cache_latent, cache_rope, home_offset, lengths):
    height, heads, width = q_latent.shape
    cells, rope = cache_rope.shape
    rows = height * heads
    aux = pack_aux(q_rope, home_offset, lengths)
    flat = q_latent.reshape(rows, width)
    n = 2 * HOPS
    dma = pltpu.SemaphoreType.DMA
    out = pl.pallas_call(
        functools.partial(window_kernel, size),
        out_shape=jax.ShapeDtypeStruct((rows, width), jnp.float32),
        in_specs=[pl.BlockSpec(memory_space=pltpu.VMEM)] * 4,
        out_specs=pl.BlockSpec(memory_space=pltpu.VMEM),
        scratch_shapes=[
            pltpu.VMEM((cells, 2 * width + 4 * rope), jnp.bfloat16),
            pltpu.VMEM((width, cells), jnp.bfloat16),
            pltpu.VMEM((width, cells), jnp.bfloat16),
            pltpu.VMEM((cells, 2 * rows), jnp.float32),
            pltpu.VMEM((cells, 2 * rows), jnp.bfloat16),
            pltpu.VMEM((cells, 2 * rows), jnp.bfloat16),
            pltpu.VMEM((n, rows, width), jnp.float32),
            pltpu.VMEM((n, heads + 8, rows), jnp.float32),
            pltpu.VMEM((n + 1, width, rows), jnp.float32),
            pltpu.VMEM((n + 1, 8, rows), jnp.float32),
            pltpu.VMEM((n, width, rows), jnp.float32),
            pltpu.VMEM((n, 8, rows), jnp.float32),
        ]
        + [dma((n,))] * 8,
        compiler_params=pltpu.CompilerParams(
            collective_id=0, has_side_effects=True, vmem_limit_bytes=60 * 1024 * 1024
        ),
    )(flat, aux, cache_latent, cache_rope)
    return out.reshape(height, heads, width)


def solution(mesh):
    return jax.shard_map(
        functools.partial(shards, mesh.shape["blk"]),
        mesh=mesh,
        in_specs=(
            P(("groups", "blk"), "head", None),
            P(("groups", "blk"), "head", None),
            P(("groups", "blk"), None),
            P(("groups", "blk"), None),
            P(("groups", "blk")),
            P(("groups", "blk")),
        ),
        out_specs=P(("groups", "blk"), "head", None),
        check_vma=False,
    )
```

time: 221 us -> 89.4 us (0.40); the launches traced: 218 us -> 89.1 us
  Pallas kernels: 0 us -> 82.6 us
  starting transfers between devices: 77.6 us -> 0 us
  matrix products: 62.2 us -> 0 us
  waiting for transfers between devices: 58.3 us -> 0 us
  other arithmetic: 16.3 us -> 1.39 us
    pallas_call x0 -> x1, Pallas kernels: none -> 82.6 us  [shards(): pl.pallas_call(functools.partial(window_kernel, size), out_shape=jax.Shap...]
    ppermute x48 -> x0, starting transfers between devices: 77.6 us -> none  [from_behind(): return lax.ppermute(x, axis, [(i, (i + by) % size) for i in range(size)])]
    dot_general x12 -> x0, matrix products: 62.2 us -> none  [the longest x4 31.5 us: visit_block(): jnp.dot(flat_query, latent_cache.T, precision=precise)]
    ppermute x48 -> x0, waiting for transfers between devices: 58.3 us -> none  [from_behind(): return lax.ppermute(x, axis, [(i, (i + by) % size) for i in range(size)])]
    reduce_sum x4 -> x0, other arithmetic: 9.23 us -> none  [visit_block(): totals = totals * fading + jnp.sum(weights, axis=2)]
    unnamed x12 -> x2, local copies, waits for them, and re-layouts: 0.03 us -> 4.04 us
    concatenate x9 -> x1, other arithmetic: 3.18 us -> 0.71 us  [pack_aux(): jnp.concatenate([packed, meta, jnp.zeros((6, height * heads), jnp.float32...]
  transfers between devices with their start and end apart: 48 -> 0, of which waited for: 19 -> 0; matrix products, arithmetic and copies ran while one was open for 28% -> 0% of each run, Pallas kernels for 0% -> 0%
where the time goes in v1:
time: 89.4 us; the launch traced here: 89.1 us
  Pallas kernels  82.6 us (92%)
  local copies, waits for them, and re-layouts  5.05 us (6%)
  other arithmetic  1.39 us (2%)
    pallas_call x1, Pallas kernels, shards(): pl.pallas_call(functools.partial(window_kernel, size), out_shape=jax.Shap...  82.6 us
    unnamed x2, local copies, waits for them, and re-layouts  4.04 us

profile of v1, /device:TPU:8, one launch (start us, length us, event | category | flops | bytes accessed | tf_op | source)
XLA Modules:
  0.0 89.1 jit_solution(9477699722400080286)
XLA Ops:
  0.0 0.1 pad.3.clone
  0.1 0.7 add_convert_fusion
  0.8 0.1 broadcast_in_dim.6
  0.8 0.1 reshape.10
  0.9 0.8 slice_bitcast_fusion.1
  1.7 0.7 maximum_maximum_fusion.aux_ref
  2.4 2.4 %copy.7.rope_ref = f32[2048,64]{1,0:T(8,128)} copy(f32[2048,64]{0,1:T(8,128)} %param.9) | data formatting | bytes 1048576 | tf_op args[3]
  4.8 82.6 %shard_map.64 = f32[128,512]{1,0:T(8,128)} custom-call(f32[128,512]{1,0:T(8,128)} %bitcast.9, f32[72,128]{1,0:T(8,128)} %maximum_maximum_fusion.aux_ref, f32[2048,512]{1,0:T(8,128)} %cache_ref.1, f32[2048,64]{1,0:T(8,128)} %copy.7.rope_ref), custom_call_target="tpu_custom_call" | custom-call | tf_op jit(solution)/shard_map/pallas_call | solution.py:233
  87.4 1.7 %copy.9 = f32[2,64,512]{2,1,0:T(8,128)} copy(f32[2,64,512]{2,1,0:T(8,128)} %bitcast.8) | data formatting | bytes 524288
  (1 shorter events, 0.0 us)

commit v2 on v1

--- a/solution.py
+++ b/solution.py
@@ -17,6 +17,8 @@
 DEAD = -2e30
 FACTOR = math.log2(math.e) / math.sqrt(NOPE + ROPE)
 CHUNK = 512
+STEP = 256
+EARLY = 32
 
 NT = (((1,), (1,)), ((), ()))
 
@@ -27,11 +29,13 @@
     return high, low
 
 
-def prepare_cache(cache_ref, rope_ref, kcat, vt_hi, vt_lo):
+def prepare_cache(cache_ref, rope_ref, kcat, vt_hi, vt_lo, fetch=None):
     cells, width = cache_ref.shape
-    step = 256
+    step = STEP
 
     def body(i, _):
+        if fetch is not None:
+            fetch(i).wait()
         rows = pl.ds(pl.multiple_of(i * step, step), step)
         block = cache_ref[rows, :]
         high, low = split(block)
@@ -41,7 +45,7 @@
         t_high, t_low = split(turned)
         vt_hi[:, rows] = t_high
         vt_lo[:, rows] = t_low
-        rope = rope_ref[rows, :]
+        rope = rope_ref[:, rows].T
         r_high = rope.astype(jnp.bfloat16).astype(jnp.float32)
         r_low = rope - r_high
         wide = jnp.concatenate([r_high, r_high, r_low, jnp.zeros_like(rope)], axis=1)
@@ -72,7 +76,7 @@
     rope = jnp.concatenate([rope_rows(p[1], heads) for p in parts], axis=0)
     q_cat = jnp.concatenate([q_hi, q_hi, rope], axis=1)
     starts = jnp.concatenate([p[1][heads : heads + 1, :] - p[2] for p in parts], axis=1)
-    extents = jnp.concatenate([p[1][heads + 1 : heads + 2, :] for p in parts], axis=1)
+    extents = jnp.concatenate([p[1][heads + 1 : heads + 2, :] * p[3] for p in parts], axis=1)
     ends = starts + extents
     wrapped = ends - window
     count = query.shape[0]
@@ -143,7 +147,7 @@
         window=window,
     )
     rows = q_ref.shape[0]
-    own = run([(q_ref[...], aux_ref[...], float(HOPS * cells))])
+    own = run([(q_ref[...], aux_ref[...], float(HOPS * cells), 1.0)])
     sums[2 * HOPS, :, :] = own[0]
     stats[2 * HOPS, 0:1, :] = own[1]
     stats[2 * HOPS, 1:2, :] = own[2]
@@ -161,7 +165,7 @@
                     device_id=device(1), device_id_type=MESH,
                 ).wait_recv()
             slot = HOPS + sign * (k + 1)
-            parts.append((q_got[i], aux_got[i], (slot * cells).astype(jnp.float32)))
+            parts.append((q_got[i], aux_got[i], (slot * cells).astype(jnp.float32), 1.0))
         summed, peak, total = run(parts)
         for j, sign in ((0, 1), (1, -1)):
             i = 2 * k + j
@@ -214,6 +218,208 @@
         out_ref[:, c : c + 128] = (piece / total).T
 
 
+def line_kernel(
+    size,
+    q_ref, aux_ref, cache_hbm, rope_ref, out_ref,
+    kcat, vt_hi, vt_lo, s_ref, ph_ref, pl_ref,
+    cache, q_all, aux_all, acc, across, across_got, along_got,
+    fetch_sem, own_sem,
+    qz_s, qz_r, az_s, az_r, qa_s, qa_r, qy_s, qy_r, ay_s, ay_r, early_s,
+    oy_s, oy_r, oz_s, oz_r,
+):
+    me = lax.axis_index("blk")
+    count = size // 2
+    z, y = me // 2, lax.rem(me, 2)
+    cells, width = cache.shape
+    rows = q_ref.shape[0]
+    window = (2 * HOPS + 1) * cells
+    partner = {"blk": me + 1 - 2 * y}
+
+    def at(zz):
+        return {"blk": 2 * zz + y}
+
+    def remote(source, target, send, recv, device):
+        return pltpu.make_async_remote_copy(
+            src_ref=source, dst_ref=target, send_sem=send, recv_sem=recv,
+            device_id=device, device_id_type=MESH,
+        )
+
+    def source_row(j):
+        near = jnp.minimum(z, count - 1 - z)
+        both = j < 2 * near
+        distance = jnp.where(both, j // 2 + 1, j - near + 1)
+        upward = jnp.where(both, lax.rem(j, 2) == 0, z < count - 1 - z)
+        return jnp.where(upward, z + distance, z - distance)
+
+    def q_along(zz, side):
+        target = at(lax.rem(z + 1 - 2 * side + count, count))
+        return (
+            remote(q_all.at[zz, 0], q_all.at[zz, 0], qz_s.at[side, zz], qz_r.at[zz], target),
+            remote(aux_all.at[zz, 0], aux_all.at[zz, 0], az_s.at[side, zz], az_r.at[zz], target),
+        )
+
+    early_rows, late_rows = pl.ds(0, EARLY), pl.ds(EARLY, rows - EARLY)
+
+    def early_along(zz, side):
+        piece = q_all.at[zz, 1, early_rows]
+        return remote(piece, piece, qa_s.at[side, zz], qa_r.at[zz], at(lax.rem(z + 1 - 2 * side + count, count)))
+
+    def q_across(zz):
+        return (
+            remote(
+                q_all.at[zz, 0, late_rows], q_all.at[zz, 1, late_rows],
+                qy_s.at[zz], qy_r.at[zz], partner,
+            ),
+            remote(aux_all.at[zz, 0], aux_all.at[zz, 1], ay_s.at[zz], ay_r.at[zz], partner),
+        )
+
+    def early_across():
+        return remote(
+            q_all.at[z, 0, early_rows], q_all.at[z, 1, early_rows], early_s.at[0], qa_r.at[z],
+            partner,
+        )
+
+    def sum_across(zz):
+        return remote(across.at[zz], across_got.at[zz], oy_s.at[zz], oy_r.at[zz], partner)
+
+    def sum_along(zz):
+        return remote(acc.at[zz], along_got.at[z], oz_s.at[zz], oz_r.at[z], at(zz))
+
+    def sum_from(zz):
+        return remote(acc.at[zz], along_got.at[zz], oz_s.at[zz], oz_r.at[zz], at(zz))
+
+    def fetch(i):
+        part = pl.ds(pl.multiple_of(i * STEP, STEP), STEP)
+        return pltpu.make_async_copy(cache_hbm.at[part], cache.at[part], fetch_sem.at[i])
+
+    own_copies = (
+        pltpu.make_async_copy(q_ref, q_all.at[z, 0], own_sem.at[0]),
+        pltpu.make_async_copy(aux_ref, aux_all.at[z, 0], own_sem.at[1]),
+    )
+    for copy in own_copies:
+        copy.start()
+    for i in range(cells // STEP):
+        fetch(i).start()
+
+    barrier = pltpu.get_barrier_semaphore()
+    pl.semaphore_signal(barrier, inc=1, device_id=partner, device_id_type=MESH)
+    for k in range(1, count):
+        other = at(lax.rem(z + k, count))
+        pl.semaphore_signal(barrier, inc=1, device_id=other, device_id_type=MESH)
+    for copy in own_copies:
+        copy.wait()
+    pl.semaphore_wait(barrier, count)
+
+    def sides(zz, action):
+        @pl.when((z < count - 1) & (zz <= z))
+        def _():
+            action(0)
+
+        @pl.when((z > 0) & (zz >= z))
+        def _():
+            action(1)
+
+    def start_along(side, zz):
+        for copy in q_along(zz, side):
+            copy.start()
+
+    early_across().start()
+    sides(z, functools.partial(start_along, zz=z))
+    for copy in q_across(z):
+        copy.start()
+
+    prepare_cache(cache, rope_ref, kcat, vt_hi, vt_lo, fetch)
+    early_across().wait_recv()
+    sides(z, lambda side: early_along(z, side).start())
+
+    def pass_on(zz):
+        for copy in q_along(zz, 0):
+            copy.wait_recv()
+        sides(zz, functools.partial(start_along, zz=zz))
+        for copy in q_across(zz):
+            copy.start()
+        early_along(zz, 0).wait_recv()
+        sides(zz, lambda side: early_along(zz, side).start())
+
+    def compute(zz):
+        for copy in q_across(zz):
+            copy.wait_recv()
+        parts = []
+        for c in range(2):
+            block = 2 * zz + (y if c == 0 else 1 - y)
+            slot = lax.rem(me - block + HOPS + size, size)
+            alive = jnp.where(slot <= 2 * HOPS, 1.0, 0.0).astype(jnp.float32)
+            parts.append((q_all[zz, c], aux_all[zz, c], (slot * cells).astype(jnp.float32), alive))
+        summed, peak, total = visit(
+            parts, kcat, vt_hi, vt_lo, s_ref, ph_ref, pl_ref, window
+        )
+        for ref, lanes in ((across, slice(rows, 2 * rows)), (acc, slice(0, rows))):
+            ref[zz, 0:width, :] = summed[:, lanes]
+            ref[zz, width : width + 8, :] = jnp.concatenate(
+                [peak[:, lanes], total[:, lanes], jnp.zeros((6, rows), jnp.float32)], axis=0
+            )
+        sum_across(zz).start()
+
+    def merge(zz, got, k):
+        first, second = acc[zz, width : width + 1, :], got[k, width : width + 1, :]
+        peak = jnp.maximum(first, second)
+        first, second = jnp.exp2(first - peak), jnp.exp2(second - peak)
+        total = acc[zz, width + 1 : width + 2, :] * first
+        total += got[k, width + 1 : width + 2, :] * second
+        acc[zz, 0:width, :] = acc[zz, 0:width, :] * first + got[k, 0:width, :] * second
+        acc[zz, width : width + 1, :] = peak
+        acc[zz, width + 1 : width + 2, :] = total
+
+    def step(i, _):
+        @pl.when(i < count - 1)
+        def _():
+            pass_on(source_row(i))
+
+        @pl.when(i < count)
+        def _():
+            compute(jnp.where(i == 0, z, source_row(i - 1)))
+
+        @pl.when(i >= 1)
+        def _():
+            zz = jnp.where(i == 1, z, source_row(i - 2))
+            sum_across(zz).wait_recv()
+            merge(zz, across_got, zz)
+
+            @pl.when(i >= 2)
+            def _():
+                sum_along(zz).start()
+
+        return 0
+
+    lax.fori_loop(0, count + 1, step, 0)
+
+    def gather(j, _):
+        zz = source_row(j)
+        sum_from(zz).wait_recv()
+        merge(z, along_got, zz)
+        return 0
+
+    lax.fori_loop(0, count - 1, gather, 0)
+    total = acc[z, width + 1 : width + 2, :]
+    for c in range(0, width, 128):
+        out_ref[:, c : c + 128] = (acc[z, c : c + 128, :] / total).T
+
+    def finish(side, zz):
+        for copy in q_along(zz, side):
+            copy.wait_send()
+        early_along(zz, side).wait_send()
+
+    early_across().wait_send()
+    for k in range(count):
+        zz = lax.rem(z + k, count)
+        sides(zz, functools.partial(finish, zz=zz))
+        for copy in q_across(zz):
+            copy.wait_send()
+        sum_across(zz).wait_send()
+        if k > 0:
+            sum_along(zz).wait_send()
+
+
 def pack_aux(q_rope, home_offset, lengths):
     height, heads, rope = q_rope.shape
     packed = jnp.concatenate([q_rope[i] for i in range(height)], axis=1)
@@ -228,32 +434,51 @@
     rows = height * heads
     aux = pack_aux(q_rope, home_offset, lengths)
     flat = q_latent.reshape(rows, width)
-    n = 2 * HOPS
+    rope_turned = cache_rope.T
     dma = pltpu.SemaphoreType.DMA
-    out = pl.pallas_call(
-        functools.partial(window_kernel, size),
-        out_shape=jax.ShapeDtypeStruct((rows, width), jnp.float32),
-        in_specs=[pl.BlockSpec(memory_space=pltpu.VMEM)] * 4,
-        out_specs=pl.BlockSpec(memory_space=pltpu.VMEM),
-        scratch_shapes=[
-            pltpu.VMEM((cells, 2 * width + 4 * rope), jnp.bfloat16),
-            pltpu.VMEM((width, cells), jnp.bfloat16),
-            pltpu.VMEM((width, cells), jnp.bfloat16),
-            pltpu.VMEM((cells, 2 * rows), jnp.float32),
-            pltpu.VMEM((cells, 2 * rows), jnp.bfloat16),
-            pltpu.VMEM((cells, 2 * rows), jnp.bfloat16),
+    vmem, anywhere = (pl.BlockSpec(memory_space=m) for m in (pltpu.VMEM, pl.ANY))
+    working = [
+        pltpu.VMEM((cells, 2 * width + 4 * rope), jnp.bfloat16),
+        pltpu.VMEM((width, cells), jnp.bfloat16),
+        pltpu.VMEM((width, cells), jnp.bfloat16),
+        pltpu.VMEM((cells, 2 * rows), jnp.float32),
+        pltpu.VMEM((cells, 2 * rows), jnp.bfloat16),
+        pltpu.VMEM((cells, 2 * rows), jnp.bfloat16),
+    ]
+    if size == 2 * HOPS + 2:
+        kernel = line_kernel
+        n = size // 2
+        in_specs = [anywhere, anywhere, anywhere, vmem]
+        scratch = [
+            pltpu.VMEM((cells, width), jnp.float32),
+            pltpu.VMEM((n, 2, rows, width), jnp.float32),
+            pltpu.VMEM((n, 2, heads + 8, rows), jnp.float32),
+        ]
+        scratch += [pltpu.VMEM((n, width + 8, rows), jnp.float32)] * 4
+        scratch += [dma((cells // STEP,)), dma((2,))]
+        scratch += [dma((2, n)), dma((n,))] * 3 + [dma((n,))] * 4 + [dma((1,))] + [dma((n,))] * 4
+    else:
+        kernel = window_kernel
+        n = 2 * HOPS
+        in_specs = [vmem] * 4
+        scratch = [
             pltpu.VMEM((n, rows, width), jnp.float32),
             pltpu.VMEM((n, heads + 8, rows), jnp.float32),
             pltpu.VMEM((n + 1, width, rows), jnp.float32),
             pltpu.VMEM((n + 1, 8, rows), jnp.float32),
             pltpu.VMEM((n, width, rows), jnp.float32),
             pltpu.VMEM((n, 8, rows), jnp.float32),
-        ]
-        + [dma((n,))] * 8,
+        ] + [dma((n,))] * 8
+    out = pl.pallas_call(
+        functools.partial(kernel, size),
+        out_shape=jax.ShapeDtypeStruct((rows, width), jnp.float32),
+        in_specs=in_specs,
+        out_specs=vmem,
+        scratch_shapes=working + scratch,
         compiler_params=pltpu.CompilerParams(
             collective_id=0, has_side_effects=True, vmem_limit_bytes=60 * 1024 * 1024
         ),
-    )(flat, aux, cache_latent, cache_rope)
+    )(flat, aux, cache_latent, rope_turned)
     return out.reshape(height, heads, width)
 
 

time: 89.4 us -> 84.8 us (0.949)
  the two profiles are of different devices: /device:TPU:8 before, /device:TPU:0 now
where the time goes in v2:
time: 84.8 us; the launch traced here: 84.5 us
  Pallas kernels  80.4 us (95%)
  local copies, waits for them, and re-layouts  2.69 us (3%)
  other arithmetic  1.39 us (2%)
    pallas_call x1, Pallas kernels, shards(): pl.pallas_call(functools.partial(kernel, size), out_shape=jax.ShapeDtypeS...  80.4 us

profile of v2, /device:TPU:0, one launch (start us, length us, event | category | flops | bytes accessed | tf_op | source)
XLA Modules:
  0.0 84.5 jit_solution(15054139083260950987)
XLA Ops:
  0.0 0.1 pad.3.clone
  0.1 0.7 add_convert_fusion
  0.8 0.1 broadcast_in_dim.6
  0.8 0.1 reshape.10
  0.9 0.8 slice_bitcast_fusion.1
  1.7 0.7 maximum_maximum_fusion.aux_ref
  2.4 80.4 %shard_map.64 = f32[128,512]{1,0:T(8,128)} custom-call(f32[128,512]{1,0:T(8,128)} %bitcast.11, f32[72,128]{1,0:T(8,128)} %maximum_maximum_fusion.aux_ref, f32[2048,512]{1,0:T(8,128)} %cache_hbm.1, f32[64,2048]{1,0:T(8,128)} %bitcast.10), custom_call_target="tpu_custom_call" | custom-call | tf_op jit(solution)/shard_map/pallas_call | solution.py:472
  82.9 1.7 %copy.8 = f32[2,64,512]{2,1,0:T(8,128)} copy(f32[2,64,512]{2,1,0:T(8,128)} %bitcast.9) | data formatting | bytes 524288
  (1 shorter events, 0.0 us)

commit v3 on v2

--- a/solution.py
+++ b/solution.py
@@ -16,9 +16,9 @@
 FLOOR = -1e30
 DEAD = -2e30
 FACTOR = math.log2(math.e) / math.sqrt(NOPE + ROPE)
-CHUNK = 512
+CHUNK = 256
 STEP = 256
-EARLY = 32
+EARLY = 64
 
 NT = (((1,), (1,)), ((), ()))
 
@@ -262,7 +262,8 @@
 
     def early_along(zz, side):
         piece = q_all.at[zz, 1, early_rows]
-        return remote(piece, piece, qa_s.at[side, zz], qa_r.at[zz], at(lax.rem(z + 1 - 2 * side + count, count)))
+        target = at(lax.rem(z + 1 - 2 * side + count, count))
+        return remote(piece, piece, qa_s.at[side, zz], qa_r.at[zz], target)
 
     def q_across(zz):
         return (
@@ -279,14 +280,25 @@
             partner,
         )
 
-    def sum_across(zz):
-        return remote(across.at[zz], across_got.at[zz], oy_s.at[zz], oy_r.at[zz], partner)
-
-    def sum_along(zz):
-        return remote(acc.at[zz], along_got.at[z], oz_s.at[zz], oz_r.at[z], at(zz))
-
-    def sum_from(zz):
-        return remote(acc.at[zz], along_got.at[zz], oz_s.at[zz], oz_r.at[zz], at(zz))
+    half = width // 2
+
+    def sum_across(zz, h):
+        return remote(
+            across.at[zz, h], across_got.at[zz, h], oy_s.at[zz, h], oy_r.at[zz, h], partner
+        )
+
+    def sum_along(zz, h):
+        return remote(acc.at[zz, h], along_got.at[z, h], oz_s.at[zz, h], oz_r.at[z, h], at(zz))
+
+    def sum_straight(zz, h):
+        device = {"blk": 2 * zz + 1 - y}
+        return remote(across.at[zz, h], along_got.at[z, h], oz_s.at[zz, h], oz_r.at[z, h], device)
+
+    def sum_from(zz, h):
+        return remote(acc.at[zz, h], along_got.at[zz, h], oz_s.at[zz, h], oz_r.at[zz, h], at(zz))
+
+    def opposite(zz):
+        return 2 * jnp.abs(z - zz) == count
 
     def fetch(i):
         part = pl.ds(pl.multiple_of(i * STEP, STEP), STEP)
@@ -354,21 +366,32 @@
             parts, kcat, vt_hi, vt_lo, s_ref, ph_ref, pl_ref, window
         )
         for ref, lanes in ((across, slice(rows, 2 * rows)), (acc, slice(0, rows))):
-            ref[zz, 0:width, :] = summed[:, lanes]
-            ref[zz, width : width + 8, :] = jnp.concatenate(
+            extra = jnp.concatenate(
                 [peak[:, lanes], total[:, lanes], jnp.zeros((6, rows), jnp.float32)], axis=0
             )
-        sum_across(zz).start()
-
-    def merge(zz, got, k):
-        first, second = acc[zz, width : width + 1, :], got[k, width : width + 1, :]
+            for h in range(2):
+                ref[zz, h, 0:half, :] = summed[h * half : (h + 1) * half, lanes]
+                ref[zz, h, half : half + 8, :] = extra
+
+        @pl.when(opposite(zz))
+        def _():
+            for h in range(2):
+                sum_straight(zz, h).start()
+
+        @pl.when(jnp.logical_not(opposite(zz)))
+        def _():
+            for h in range(2):
+                sum_across(zz, h).start()
+
+    def merge(zz, got, k, h):
+        first, second = acc[zz, h, half : half + 1, :], got[k, h, half : half + 1, :]
         peak = jnp.maximum(first, second)
         first, second = jnp.exp2(first - peak), jnp.exp2(second - peak)
-        total = acc[zz, width + 1 : width + 2, :] * first
-        total += got[k, width + 1 : width + 2, :] * second
-        acc[zz, 0:width, :] = acc[zz, 0:width, :] * first + got[k, 0:width, :] * second
-        acc[zz, width : width + 1, :] = peak
-        acc[zz, width + 1 : width + 2, :] = total
+        total = acc[zz, h, half + 1 : half + 2, :] * first
+        total += got[k, h, half + 1 : half + 2, :] * second
+        acc[zz, h, 0:half, :] = acc[zz, h, 0:half, :] * first + got[k, h, 0:half, :] * second
+        acc[zz, h, half : half + 1, :] = peak
+        acc[zz, h, half + 1 : half + 2, :] = total
 
     def step(i, _):
         @pl.when(i < count - 1)
@@ -382,12 +405,16 @@
         @pl.when(i >= 1)
         def _():
             zz = jnp.where(i == 1, z, source_row(i - 2))
-            sum_across(zz).wait_recv()
-            merge(zz, across_got, zz)
-
-            @pl.when(i >= 2)
+
+            @pl.when(jnp.logical_not(opposite(zz)))
             def _():
-                sum_along(zz).start()
+                for h in range(2):
+                    sum_across(zz, h).wait_recv()
+                    merge(zz, across_got, zz, h)
+
+                    @pl.when(i >= 2)
+                    def _():
+                        sum_along(zz, h).start()
 
         return 0
 
@@ -395,14 +422,16 @@
 
     def gather(j, _):
         zz = source_row(j)
-        sum_from(zz).wait_recv()
-        merge(z, along_got, zz)
+        for h in range(2):
+            sum_from(zz, h).wait_recv()
+            merge(z, along_got, zz, h)
         return 0
 
     lax.fori_loop(0, count - 1, gather, 0)
-    total = acc[z, width + 1 : width + 2, :]
+    total = acc[z, 0, half + 1 : half + 2, :]
     for c in range(0, width, 128):
-        out_ref[:, c : c + 128] = (acc[z, c : c + 128, :] / total).T
+        h, r = divmod(c, half)
+        out_ref[:, c : c + 128] = (acc[z, h, r : r + 128, :] / total).T
 
     def finish(side, zz):
         for copy in q_along(zz, side):
@@ -415,9 +444,18 @@
         sides(zz, functools.partial(finish, zz=zz))
         for copy in q_across(zz):
             copy.wait_send()
-        sum_across(zz).wait_send()
-        if k > 0:
-            sum_along(zz).wait_send()
+
+        @pl.when(opposite(zz))
+        def _():
+            for h in range(2):
+                sum_straight(zz, h).wait_send()
+
+        @pl.when(jnp.logical_not(opposite(zz)))
+        def _():
+            for h in range(2):
+                sum_across(zz, h).wait_send()
+                if k > 0:
+                    sum_along(zz, h).wait_send()
 
 
 def pack_aux(q_rope, home_offset, lengths):
@@ -454,9 +492,9 @@
             pltpu.VMEM((n, 2, rows, width), jnp.float32),
             pltpu.VMEM((n, 2, heads + 8, rows), jnp.float32),
         ]
-        scratch += [pltpu.VMEM((n, width + 8, rows), jnp.float32)] * 4
+        scratch += [pltpu.VMEM((n, 2, width // 2 + 8, rows), jnp.float32)] * 4
         scratch += [dma((cells // STEP,)), dma((2,))]
-        scratch += [dma((2, n)), dma((n,))] * 3 + [dma((n,))] * 4 + [dma((1,))] + [dma((n,))] * 4
+        scratch += [dma((2, n)), dma((n,))] * 3 + [dma((n,))] * 4 + [dma((1,))] + [dma((n, 2))] * 4
     else:
         kernel = window_kernel
         n = 2 * HOPS

time: 84.8 us -> 75.7 us (0.89)
  the two profiles are of different devices: /device:TPU:0 before, /device:TPU:8 now
where the time goes in v3:
time: 75.7 us; the launch traced here: 75.5 us
  Pallas kernels  71.4 us (94%)
  local copies, waits for them, and re-layouts  2.69 us (4%)
  other arithmetic  1.39 us (2%)
    pallas_call x1, Pallas kernels, shards(): pl.pallas_call(functools.partial(kernel, size), out_shape=jax.ShapeDtypeS...  71.4 us
    unnamed x1, local copies, waits for them, and re-layouts  1.67 us

profile of v3, /device:TPU:8, one launch (start us, length us, event | category | flops | bytes accessed | tf_op | source)
XLA Modules:
  0.0 75.5 jit_solution(16196278010277953089)
XLA Ops:
  0.0 0.1 pad.3.clone
  0.1 0.7 add_convert_fusion
  0.8 0.1 broadcast_in_dim.6
  0.8 0.1 reshape.10
  0.9 0.8 %slice_bitcast_fusion.1 = (f32[64,64]{1,0:T(8,128)S(1)}, f32[64,64]{1,0:T(8,128)S(1)}) fusion(f32[2,64,64]{2,1,0:T(8,128)} %param.7), kind=kLoop, calls=%fused_computation.2 | loop fusion | bytes 65536 | tf_op jit(solution)/shard_map/squeeze | solution.py:463
  1.7 0.7 maximum_maximum_fusion.aux_ref
  2.4 71.4 %shard_map.64 = f32[128,512]{1,0:T(8,128)} custom-call(f32[128,512]{1,0:T(8,128)} %bitcast.11, f32[72,128]{1,0:T(8,128)} %maximum_maximum_fusion.aux_ref, f32[2048,512]{1,0:T(8,128)} %cache_hbm.1, f32[64,2048]{1,0:T(8,128)} %bitcast.10), custom_call_target="tpu_custom_call" | custom-call | tf_op jit(solution)/shard_map/pallas_call | solution.py:510
  73.8 1.7 %copy.8 = f32[2,64,512]{2,1,0:T(8,128)} copy(f32[2,64,512]{2,1,0:T(8,128)} %bitcast.9) | data formatting | bytes 524288
  (1 shorter events, 0.0 us)

commit v4 on v3

--- a/solution.py
+++ b/solution.py
@@ -224,7 +224,7 @@
     kcat, vt_hi, vt_lo, s_ref, ph_ref, pl_ref,
     cache, q_all, aux_all, acc, across, across_got, along_got,
     fetch_sem, own_sem,
-    qz_s, qz_r, az_s, az_r, qa_s, qa_r, qy_s, qy_r, ay_s, ay_r, early_s,
+    qz_s, qz_r, qe_s, qe_r, az_s, az_r, qa_s, qa_r, qy_s, qy_r, ay_s, ay_r, early_s,
     oy_s, oy_r, oz_s, oz_r,
 ):
     me = lax.axis_index("blk")
@@ -251,14 +251,20 @@
         upward = jnp.where(both, lax.rem(j, 2) == 0, z < count - 1 - z)
         return jnp.where(upward, z + distance, z - distance)
 
+    early_rows, late_rows = pl.ds(0, EARLY), pl.ds(EARLY, rows - EARLY)
+
     def q_along(zz, side):
         target = at(lax.rem(z + 1 - 2 * side + count, count))
+        piece = q_all.at[zz, 0, late_rows]
         return (
-            remote(q_all.at[zz, 0], q_all.at[zz, 0], qz_s.at[side, zz], qz_r.at[zz], target),
+            remote(piece, piece, qz_s.at[side, zz], qz_r.at[zz], target),
             remote(aux_all.at[zz, 0], aux_all.at[zz, 0], az_s.at[side, zz], az_r.at[zz], target),
         )
 
-    early_rows, late_rows = pl.ds(0, EARLY), pl.ds(EARLY, rows - EARLY)
+    def rest_along(zz, side):
+        target = at(lax.rem(z + 1 - 2 * side + count, count))
+        piece = q_all.at[zz, 0, early_rows]
+        return remote(piece, piece, qe_s.at[side, zz], qe_r.at[zz], target)
 
     def early_along(zz, side):
         piece = q_all.at[zz, 1, early_rows]
@@ -331,6 +337,17 @@
         def _():
             action(1)
 
+    def unused(zz, row):
+        return (2 * jnp.abs(row - zz) == count) & ((row == 0) | (row == count - 1))
+
+    def rest_sides(zz, action):
+        def guarded(side):
+            @pl.when(jnp.logical_not(unused(zz, z + 1 - 2 * side)))
+            def _():
+                action(side)
+
+        sides(zz, guarded)
+
     def start_along(side, zz):
         for copy in q_along(zz, side):
             copy.start()
@@ -339,6 +356,7 @@
     sides(z, functools.partial(start_along, zz=z))
     for copy in q_across(z):
         copy.start()
+    rest_sides(z, lambda side: rest_along(z, side).start())
 
     prepare_cache(cache, rope_ref, kcat, vt_hi, vt_lo, fetch)
     early_across().wait_recv()
@@ -350,6 +368,12 @@
         sides(zz, functools.partial(start_along, zz=zz))
         for copy in q_across(zz):
             copy.start()
+
+        @pl.when(jnp.logical_not(unused(zz, z)))
+        def _():
+            rest_along(zz, 0).wait_recv()
+            rest_sides(zz, lambda side: rest_along(zz, side).start())
+
         early_along(zz, 0).wait_recv()
         sides(zz, lambda side: early_along(zz, side).start())
 
@@ -442,6 +466,7 @@
     for k in range(count):
         zz = lax.rem(z + k, count)
         sides(zz, functools.partial(finish, zz=zz))
+        rest_sides(zz, lambda side: rest_along(zz, side).wait_send())
         for copy in q_across(zz):
             copy.wait_send()
 
@@ -494,7 +519,7 @@
         ]
         scratch += [pltpu.VMEM((n, 2, width // 2 + 8, rows), jnp.float32)] * 4
         scratch += [dma((cells // STEP,)), dma((2,))]
-        scratch += [dma((2, n)), dma((n,))] * 3 + [dma((n,))] * 4 + [dma((1,))] + [dma((n, 2))] * 4
+        scratch += [dma((2, n)), dma((n,))] * 4 + [dma((n,))] * 4 + [dma((1,))] + [dma((n, 2))] * 4
     else:
         kernel = window_kernel
         n = 2 * HOPS

time: 75.7 us -> 74.1 us (0.979)
  Pallas kernels: 71.4 us -> 69.7 us
    pallas_call x1, Pallas kernels: 71.4 us -> 69.7 us  [shards(): pl.pallas_call(functools.partial(kernel, size), out_shape=jax.ShapeDtypeS...]
where the time goes in v4:
time: 74.1 us; the launch traced here: 73.8 us
  Pallas kernels  69.7 us (94%)
  local copies, waits for them, and re-layouts  2.69 us (4%)
  other arithmetic  1.39 us (2%)
    pallas_call x1, Pallas kernels, shards(): pl.pallas_call(functools.partial(kernel, size), out_shape=jax.ShapeDtypeS...  69.7 us
    unnamed x1, local copies, waits for them, and re-layouts  1.67 us

profile of v4, /device:TPU:8, one launch (start us, length us, event | category | flops | bytes accessed | tf_op | source)
XLA Modules:
  0.0 73.8 jit_solution(4970800070211784927)
XLA Ops:
  0.0 0.1 pad.3.clone
  0.1 0.7 add_convert_fusion
  0.8 0.1 broadcast_in_dim.6
  0.8 0.1 reshape.10
  0.9 0.8 %slice_bitcast_fusion.1 = (f32[64,64]{1,0:T(8,128)S(1)}, f32[64,64]{1,0:T(8,128)S(1)}) fusion(f32[2,64,64]{2,1,0:T(8,128)} %param.7), kind=kLoop, calls=%fused_computation.2 | loop fusion | bytes 65536 | tf_op jit(solution)/shard_map/squeeze | solution.py:488
  1.7 0.7 maximum_maximum_fusion.aux_ref
  2.4 69.7 %shard_map.64 = f32[128,512]{1,0:T(8,128)} custom-call(f32[128,512]{1,0:T(8,128)} %bitcast.11, f32[72,128]{1,0:T(8,128)} %maximum_maximum_fusion.aux_ref, f32[2048,512]{1,0:T(8,128)} %cache_hbm.1, f32[64,2048]{1,0:T(8,128)} %bitcast.10), custom_call_target="tpu_custom_call" | custom-call | tf_op jit(solution)/shard_map/pallas_call | solution.py:535
  72.1 1.7 %copy.8 = f32[2,64,512]{2,1,0:T(8,128)} copy(f32[2,64,512]{2,1,0:T(8,128)} %bitcast.9) | data formatting | bytes 524288
  (1 shorter events, 0.0 us)
